TPU v7x, 32 devices: a whole 2x2x4 slice. The times are simulated.
32 devices in a mesh: section: 4 (over y, x), dp: 2 (over core), mp: 4 (over z).
Axes of the slice: x: 2, y: 2, z: 4, core: 2. Of those that a mesh axis runs over, the one named last changes fastest.
Arguments:
- act_sent: bfloat16 [4, 16, 3072], P('section', ('dp', 'mp')), may hold values from -6 to 6
- new_batch: bfloat16 [16, 3072], P(('dp', 'mp')), may hold values from -6 to 6
- saved_input: bfloat16 [4, 16, 3072], P('section', ('dp', 'mp')), may hold values from -6 to 6
- grad_sent: bfloat16 [4, 16, 3072], P('section', ('dp', 'mp')), may hold values from -6 to 6
- loss_grad: bfloat16 [16, 3072], P(('dp', 'mp')), may hold values from -6 to 6
- ln_gain: float32 [4, 3072], P('section'), may hold values from 0.1 to 1.9
- w_in: bfloat16 [4, 3072, 16384], P('section', None, 'mp'), may hold values from -0.109375 to 0.109375
- w_out: bfloat16 [4, 3072, 16384], P('section', None, 'mp'), may hold values from -0.046875 to 0.046875
Outputs:
- act_out: bfloat16 [4, 16, 3072], P('section', ('dp', 'mp'))
- grad_out: bfloat16 [4, 16, 3072], P('section', ('dp', 'mp'))
- grad_w_in: bfloat16 [4, 3072, 16384], P('section', 'dp', 'mp')
- grad_w_out: bfloat16 [4, 3072, 16384], P('section', 'dp', 'mp')
All inputs are finite; a program needn't handle non-finite values.
Results may differ from a plain program's by a relative error of at most 0.0075.
Values may be sent and summed in bfloat16 or wider, within the bound.
No kernel may reach another device: no remote copies, remote signals or barrier semaphores. Data moves between devices by JAX's collectives and lax.ppermute only.
A program may use at most 128 MiB of HBM per device.

v0:
```python
import jax
import jax.numpy as jnp
from jax import lax
from jax.sharding import PartitionSpec as P

gelu_c = 0.7978845608028654


def from_behind(block, axis, distance):
    devices = range(lax.axis_size(axis))
    route = [(i - distance, i) for i in devices if i - distance in devices]
    return lax.ppermute(block, axis, route)


def gelu_pair(h):
    inner = gelu_c * (h + 0.044715 * h * h * h)
    tval = jnp.tanh(inner)
    value = 0.5 * h * (1.0 + tval)
    slope = 0.5 * (1.0 + tval) + 0.5 * h * (1.0 - tval * tval) * gelu_c * (
        1.0 + 3.0 * 0.044715 * h * h
    )
    return (value, slope)


def normalize(rows):
    xval = rows.astype(jnp.float32)
    centre = xval - jnp.mean(xval, axis=-1, keepdims=True)
    rstd = lax.rsqrt(jnp.mean(centre * centre, axis=-1, keepdims=True) + 1e-05)
    return (centre * rstd, rstd)


def contract_rows(left, right):
    return lax.dot_general(
        left, right, (((0,), (0,)), ((), ())), preferred_element_type=jnp.float32
    )


def per_device(act_sent, new_batch, saved_input, grad_sent, loss_grad, ln_gain, w_in, w_out):
    section_idx = lax.axis_index("section")
    sections = lax.axis_size("section")
    arrived = from_behind(act_sent, "section", 1)
    returned = from_behind(grad_sent, "section", -1)
    x_fwd = jnp.where(section_idx == 0, new_batch, arrived[0])
    upstream = jnp.where(section_idx == sections - 1, loss_grad, returned[0])
    gain = ln_gain[0]
    nhat_fwd, _ = normalize(x_fwd)
    n_fwd = (nhat_fwd * gain).astype(jnp.bfloat16)
    nhat_bwd, rstd_bwd = normalize(saved_input[0])
    n_bwd = (nhat_bwd * gain).astype(jnp.bfloat16)
    rows_fwd, rows_bwd, rows_up = (
        lax.all_gather(n_fwd, "mp", axis=0, tiled=True),
        lax.all_gather(n_bwd, "mp", axis=0, tiled=True),
        lax.all_gather(upstream, "mp", axis=0, tiled=True),
    )
    weight_in = w_in[0]
    weight_out = w_out[0]
    h_fwd = jnp.dot(rows_fwd, weight_in, preferred_element_type=jnp.float32)
    g_fwd = gelu_pair(h_fwd)[0].astype(jnp.bfloat16)
    branch_part = lax.dot_general(
        g_fwd, weight_out, (((1,), (1,)), ((), ())), preferred_element_type=jnp.float32
    )
    h_bwd = jnp.dot(rows_bwd, weight_in, preferred_element_type=jnp.float32)
    g_val, slope = gelu_pair(h_bwd)
    g_bwd = g_val.astype(jnp.bfloat16)
    grad_act = jnp.dot(rows_up, weight_out, preferred_element_type=jnp.float32)
    grad_hidden = (grad_act * slope).astype(jnp.bfloat16)
    norm_part = lax.dot_general(
        grad_hidden, weight_in, (((1,), (1,)), ((), ())), preferred_element_type=jnp.float32
    )
    branch_sum, grad_norm = (
        lax.psum_scatter(branch_part, "mp", scatter_dimension=0, tiled=True),
        lax.psum_scatter(norm_part, "mp", scatter_dimension=0, tiled=True),
    )
    act_out = (x_fwd.astype(jnp.float32) + branch_sum).astype(jnp.bfloat16)
    scaled = grad_norm * gain
    grad_in = upstream.astype(jnp.float32) + rstd_bwd * (
        scaled
        - jnp.mean(scaled, axis=-1, keepdims=True)
        - nhat_bwd * jnp.mean(scaled * nhat_bwd, axis=-1, keepdims=True)
    )
    all_norm, all_up, all_act, all_hidden = (
        lax.all_gather(rows_bwd, "dp", axis=0, tiled=True),
        lax.all_gather(rows_up, "dp", axis=0, tiled=True),
        lax.all_gather(g_bwd, "dp", axis=0, tiled=True),
        lax.all_gather(grad_hidden, "dp", axis=0, tiled=True),
    )
    replicas = lax.axis_size("dp")
    half = weight_in.shape[0] // replicas
    start = lax.axis_index("dp") * half
    cols_norm = lax.dynamic_slice_in_dim(all_norm, start, half, 1)
    cols_up = lax.dynamic_slice_in_dim(all_up, start, half, 1)
    block = rows_bwd.shape[0]
    sum_in = jnp.zeros((half, weight_in.shape[1]), jnp.float32)
    sum_out = jnp.zeros((half, weight_in.shape[1]), jnp.float32)
    for replica in range(replicas):
        low = replica * block
        term_in = contract_rows(cols_norm[low : low + block], all_hidden[low : low + block])
        term_out = contract_rows(cols_up[low : low + block], all_act[low : low + block])
        sum_in = sum_in + term_in.astype(jnp.bfloat16).astype(jnp.float32)
        sum_out = sum_out + term_out.astype(jnp.bfloat16).astype(jnp.float32)
    return (
        act_out[None],
        grad_in.astype(jnp.bfloat16)[None],
        sum_in.astype(jnp.bfloat16)[None],
        sum_out.astype(jnp.bfloat16)[None],
    )


def solution(mesh):
    return jax.shard_map(
        per_device,
        mesh=mesh,
        in_specs=(
            P("section", ("dp", "mp"), None),
            P(("dp", "mp"), None),
            P("section", ("dp", "mp"), None),
            P("section", ("dp", "mp"), None),
            P(("dp", "mp"), None),
            P("section", None),
            P("section", None, "mp"),
            P("section", None, "mp"),
        ),
        out_specs=(
            P("section", ("dp", "mp"), None),
            P("section", ("dp", "mp"), None),
            P("section", "dp", "mp"),
            P("section", "dp", "mp"),
        ),
        check_vma=False,
    )
```

profile of v0, /device:TPU:0, one launch (start us, length us, event | category | flops | bytes accessed | tf_op | source)
XLA Modules:
  0.0 181.2 jit_solution(3140549871322711195)
XLA Ops:
  7.2 0.0 all-reduce.5.cloned.1.call-start
  7.2 4.9 %collective-permute-start = (bf16[1,2,3072]{2,1,0:T(2,128)(2,1)}, bf16[1,2,3072]{2,1,0:T(2,128)(2,1)S(1)}, u32[]{:S(2)}, u32[]{:S(2)}) collective-permute-start(bf16[1,2,3072]{2,1,0:T(2,128)(2,1)} %param.8), channel_id=1, source_target_pairs={{0,8},{8,16},{16,24},{1,9},{9,17},{17,25},{2,10},{10,18},{18,26},{... | collective-permute-start | bytes 36872 | tf_op jit(solution)/shard_map/ppermute | solution.py:12
  12.1 1.3 collective-permute-start.1
  13.4 0.8 convert_reduce_fusion.1
  14.2 0.9 fusion.48
  15.2 1.2 dynamic-slice
  17.1 0.0 collective-permute-done
  17.1 0.9 convert_reduce_fusion
  17.9 0.2 fusion.42
  18.2 0.8 fusion.55
  19.0 13.4 %all-gather.2 = bf16[4,2,3072]{2,1,0:T(2,128)(2,1)S(1)} all-gather(bf16[1,2,3072]{2,1,0:T(2,128)(2,1)S(1)} %get-tuple-element.10), channel_id=1, replica_groups=mesh['section'=4,'dp'=2,'mp'=4] {'mp'}, dimensions={0}, use_global_device_ids=true | all-gather | bytes 61440 | tf_op jit(solution)/shard_map/all_gather | solution.py:52
  32.4 0.0 collective-permute-done.1
  32.4 13.1 %all-gather.1 = bf16[4,2,3072]{2,1,0:T(2,128)(2,1)S(1)} all-gather(bf16[1,2,3072]{2,1,0:T(2,128)(2,1)S(1)} %fusion.60), channel_id=1, replica_groups=mesh['section'=4,'dp'=2,'mp'=4] {'mp'}, dimensions={0}, use_global_device_ids=true | all-gather | bytes 61440 | tf_op jit(solution)/shard_map/all_gather | solution.py:53
  45.6 1.9 %all_gather.26 = bf16[16,3072]{1,0:T(8,128)(2,1)S(1)} all-gather(bf16[8,3072]{1,0:T(8,128)(2,1)S(1)} %reshape.44), channel_id=1, replica_groups=mesh['section'=4,'dp'=2,'mp'=4] {'dp'}, dimensions={0}, use_global_device_ids=true | all-gather | bytes 147456 | tf_op jit(solution)/shard_map/all_gather | solution.py:83
  47.4 1.9 %all_gather.24 = bf16[16,3072]{1,0:T(8,128)(2,1)S(1)} all-gather(bf16[8,3072]{1,0:T(8,128)(2,1)S(1)} %reshape.46), channel_id=1, replica_groups=mesh['section'=4,'dp'=2,'mp'=4] {'dp'}, dimensions={0}, use_global_device_ids=true | all-gather | bytes 147456 | tf_op jit(solution)/shard_map/all_gather | solution.py:82
  49.3 9.9 %multiply_convert_fusion = (bf16[8,4096]{1,0:T(8,128)(2,1)S(1)}, f32[8,4096]{1,0:T(8,128)S(1)}) fusion(bf16[8,3072]{1,0:T(8,128)(2,1)S(1)} %reshape.46, bf16[1,3072,4096]{2,1,0:T(8,128)(2,1)} %param.14), kind=kOutput, calls=%fused_computation.33 | convolution fusion | flops 201621504 | bytes 25411584 | tf_op jit(solution)/shard_map/dot_general | solution.py:62
  59.2 10.0 %fusion.15 = bf16[8,4096]{1,0:T(8,128)(2,1)S(1)} fusion(bf16[8,3072]{1,0:T(8,128)(2,1)S(1)} %reshape.44, bf16[1,3072,4096]{2,1,0:T(8,128)(2,1)} %param.15, f32[8,4096]{1,0:T(8,128)S(1)} %get-tuple-element.13), kind=kOutput, calls=%fused_computation.19 | convolution fusion | flops 201949184 | bytes 25411584 | tf_op jit(solution)/shard_map/dot_general | solution.py:65
  69.2 12.2 %fusion.4 = f32[8,3072]{1,0:T(8,128)} fusion(bf16[8,4096]{1,0:T(8,128)(2,1)S(1)} %fusion.15, bf16[1,3072,4096]{2,1,0:T(8,128)(2,1)} %param.14), kind=kOutput, calls=%fused_computation.4 | convolution fusion | flops 201326592 | bytes 25329664 | tf_op jit(solution)/shard_map/dot_general | solution.py:67
  81.4 1.9 %all_gather.25 = bf16[16,4096]{1,0:T(8,128)(2,1)S(1)} all-gather(bf16[8,4096]{1,0:T(8,128)(2,1)S(1)} %fusion.15), channel_id=1, replica_groups=mesh['section'=4,'dp'=2,'mp'=4] {'dp'}, dimensions={0}, use_global_device_ids=true | all-gather | bytes 196608 | tf_op jit(solution)/shard_map/all_gather | solution.py:85
  83.3 13.1 %all-gather = bf16[4,2,3072]{2,1,0:T(2,128)(2,1)S(1)} all-gather(bf16[1,2,3072]{2,1,0:T(2,128)(2,1)S(1)} %get-tuple-element.11), channel_id=1, replica_groups=mesh['section'=4,'dp'=2,'mp'=4] {'mp'}, dimensions={0}, use_global_device_ids=true | all-gather | bytes 61440 | tf_op jit(solution)/shard_map/all_gather | solution.py:51
  96.4 19.8 %fusion.2 = f32[8,3072]{1,0:T(8,128)} fusion(bf16[1,3072,4096]{2,1,0:T(8,128)(2,1)} %param.15, bf16[8,3072]{1,0:T(8,128)(2,1)S(1)} %reshape.42, bf16[1,3072,4096]{2,1,0:T(8,128)(2,1)} %param.14), kind=kOutput, calls=%fused_computation.2 | convolution fusion | flops 402948096 | bytes 50479104 | tf_op jit(solution)/shard_map/dot_general | solution.py:59
  116.1 2.1 %all_gather.27 = bf16[16,4096]{1,0:T(8,128)(2,1)S(1)} all-gather(bf16[8,4096]{1,0:T(8,128)(2,1)S(1)} %get-tuple-element.12), channel_id=1, replica_groups=mesh['section'=4,'dp'=2,'mp'=4] {'dp'}, dimensions={0}, use_global_device_ids=true | all-gather | bytes 196608 | tf_op jit(solution)/shard_map/all_gather | solution.py:84
  118.2 6.6 %convolution_convert_fusion.2 = bf16[1536,4096]{1,0:T(8,128)(2,1)} fusion(bf16[16,4096]{1,0:T(8,128)(2,1)S(1)} %all_gather.25, bf16[16,3072]{1,0:T(8,128)(2,1)S(1)} %all_gather.24, s32[]{:T(128)S(6)} %add.72, s32[]{:T(128)S(6)} %select_n.22), kind=kOutput, calls=%fused_computation.14 | convolution fusion | flops 106954752 | bytes 12673032 | tf_op jit(solution)/shard_map/dot_general | solution.py:33
  124.8 9.4 %fusion.10 = bf16[1,1536,4096]{2,1,0:T(8,128)(2,1)} fusion(bf16[1536,4096]{1,0:T(8,128)(2,1)} %convolution_convert_fusion.2, bf16[16,4096]{1,0:T(8,128)(2,1)S(1)} %all_gather.25, bf16[16,3072]{1,0:T(8,128)(2,1)S(1)} %all_gather.24, s32[]{:T(128)S(6)} %select_n.22), kind=kOutput, calls=%fused_computation.16 | convolution fusion | flops 132120576 | bytes 25255940 | tf_op jit(solution)/shard_map/dot_general | solution.py:33
  134.2 0.0 all-reduce.5.cloned.1.call-update
  134.2 0.0 copy-start
  134.2 0.0 copy-start.1
  134.3 0.0 copy-start.2
  134.3 6.6 %convolution_convert_fusion = bf16[1536,4096]{1,0:T(8,128)(2,1)} fusion(bf16[16,4096]{1,0:T(8,128)(2,1)S(1)} %all_gather.27, bf16[16,3072]{1,0:T(8,128)(2,1)S(1)} %all_gather.26, s32[]{:T(128)S(6)} %add.72, s32[]{:T(128)S(6)} %select_n.22), kind=kOutput, calls=%fused_computation.12 | convolution fusion | flops 106954752 | bytes 12673032 | tf_op jit(solution)/shard_map/dot_general | solution.py:33
  140.9 9.4 %fusion.11 = bf16[1,1536,4096]{2,1,0:T(8,128)(2,1)} fusion(bf16[1536,4096]{1,0:T(8,128)(2,1)} %convolution_convert_fusion, bf16[16,4096]{1,0:T(8,128)(2,1)S(1)} %all_gather.27, bf16[16,3072]{1,0:T(8,128)(2,1)S(1)} %all_gather.26, s32[]{:T(128)S(6)} %select_n.22), kind=kOutput, calls=%fused_computation.17 | convolution fusion | flops 132120576 | bytes 25255940 | tf_op jit(solution)/shard_map/dot_general | solution.py:33
  150.3 21.2 %all-reduce.5.cloned.1.call-done = (f32[8,3072]{1,0:T(8,128)}, f32[8,3072]{1,0:T(8,128)}) async-done(((f32[8,3072]{1,0:T(8,128)}, f32[8,3072]{1,0:T(8,128)}), (f32[8,3072]{1,0:T(8,128)}, f32[8,3072]{1,0:T(8,128)})) %all-reduce.5.cloned.1.call-update) | async-done | bytes 196624
  171.5 0.0 copy-done
  171.6 0.0 copy-done.1
  171.6 1.1 fusion.65
  172.7 0.0 copy-done.2
  172.7 1.7 fusion.54
  (10 shorter events, 0.1 us)
Async XLA Ops:
  7.2 164.4 %all-reduce.5.cloned.1.call-start = ((), (), s32[]{:S(2)}) async-start(), calls=%async_computation | async-start | bytes 393216
  7.2 9.9 %collective-permute-start = (bf16[1,2,3072]{2,1,0:T(2,128)(2,1)}, bf16[1,2,3072]{2,1,0:T(2,128)(2,1)S(1)}, u32[]{:S(2)}, u32[]{:S(2)}) collective-permute-start(bf16[1,2,3072]{2,1,0:T(2,128)(2,1)} %param.8), channel_id=1, source_target_pairs={{0,8},{8,16},{16,24},{1,9},{9,17},{17,25},{2,10},{10,18},{18,26},{... | collective-permute-start | bytes 36872 | tf_op jit(solution)/shard_map/ppermute | solution.py:12
  12.1 20.3 %collective-permute-start.1 = (bf16[1,2,3072]{2,1,0:T(2,128)(2,1)}, bf16[1,2,3072]{2,1,0:T(2,128)(2,1)S(1)}, u32[]{:S(2)}, u32[]{:S(2)}) collective-permute-start(bf16[1,2,3072]{2,1,0:T(2,128)(2,1)} %param.11), channel_id=1, source_target_pairs={{8,0},{16,8},{24,16},{9,1},{17,9},{25,17},{10,2},{18,10},{26,18},{... | collective-permute-start | bytes 36872 | tf_op jit(solution)/shard_map/ppermute | solution.py:12
  134.2 37.3 %copy-start = (bf16[1,2,3072]{2,1,0:T(2,128)(2,1)S(1)}, bf16[1,2,3072]{2,1,0:T(2,128)(2,1)}, u32[]{:S(2)}) copy-start(bf16[1,2,3072]{2,1,0:T(2,128)(2,1)} %param.10) | copy-start | bytes 36868
  134.2 37.3 %copy-start.1 = (f32[1,3072]{1,0:T(1,128)S(1)}, f32[1,3072]{1,0:T(1,128)}, u32[]{:S(2)}) copy-start(f32[1,3072]{1,0:T(1,128)} %param.13) | copy-start | bytes 36868
  134.3 38.4 %copy-start.2 = (bf16[2,3072]{1,0:T(2,128)(2,1)S(1)}, bf16[2,3072]{1,0:T(2,128)(2,1)}, u32[]{:S(2)}) copy-start(bf16[2,3072]{1,0:T(2,128)(2,1)} %param.12) | copy-start | bytes 36868
Sparse Core Ops, SparseCore 0:
  134.4 37.1 all-reduce.4
where the time goes:
time: 182 us; the launch traced here: 181 us
  matrix products  83.9 us (46%)
  blocking collectives  47.2 us (26%)
  waiting for transfers between devices  21.2 us (12%)
  between operations  14.8 us (8%)
  other arithmetic  6.5 us (4%)
  starting transfers between devices  6.2 us (3%)
    dot_general x4, matrix products, contract_rows(): lax.dot_general(left, right, (((0,), (0,)), ((), ())), preferred_element_...  32.1 us
    unnamed x2, waiting for transfers between devices  21.2 us
    dot_general x1, matrix products, per_device(): lax.dot_general(g_fwd, weight_out, (((1,), (1,)), ((), ())), preferred_el...  19.8 us
    all_gather x1, blocking collectives, per_device(): lax.all_gather(n_bwd, 'mp', axis=0, tiled=True)  13.4 us
    all_gather x1, blocking collectives, per_device(): lax.all_gather(upstream, 'mp', axis=0, tiled=True)  13.1 us
    all_gather x1, blocking collectives, per_device(): lax.all_gather(n_fwd, 'mp', axis=0, tiled=True)  13.1 us
    dot_general x1, matrix products, per_device(): lax.dot_general(grad_hidden, weight_in, (((1,), (1,)), ((), ())), preferr...  12.2 us
    dot_general x1, matrix products, per_device(): grad_act = jnp.dot(rows_up, weight_out, preferred_element_type=jnp.float32)  10 us
  transfers between devices with their start and end apart: 3, of which 1 were waited for; matrix products, arithmetic and copies ran while one was open for 12% of the time, Pallas kernels for 0%

commit v1 on v0

--- a/solution.py
+++ b/solution.py
@@ -4,6 +4,16 @@
 from jax.sharding import PartitionSpec as P
 
 gelu_c = 0.7978845608028654
+
+
+def gather_around(x, axis, dim):
+    ways, here, lap = (lax.axis_size(axis), lax.axis_index(axis), x.shape[dim])
+    shape = [n * ways if d == dim else n for d, n in enumerate(x.shape)]
+    full = lax.dynamic_update_slice_in_dim(jnp.zeros(shape, x.dtype), x, here * lap, axis=dim)
+    for far in range(1, ways):
+        x = lax.ppermute(x, axis, [(d, (d + 1) % ways) for d in range(ways)])
+        full = lax.dynamic_update_slice_in_dim(full, x, (here - far) % ways * lap, axis=dim)
+    return full
 
 
 def from_behind(block, axis, distance):
@@ -49,7 +59,7 @@
     n_bwd = (nhat_bwd * gain).astype(jnp.bfloat16)
     rows_fwd, rows_bwd, rows_up = (
         lax.all_gather(n_fwd, "mp", axis=0, tiled=True),
-        lax.all_gather(n_bwd, "mp", axis=0, tiled=True),
+        gather_around(n_bwd, "mp", 0),
         lax.all_gather(upstream, "mp", axis=0, tiled=True),
     )
     weight_in = w_in[0]

time: 182 us -> 161 us (0.88)
  blocking collectives: 47.2 us -> 34.1 us
  waiting for transfers between devices: 21.2 us -> 10.8 us
  starting transfers between devices: 6.2 us -> 8.17 us
    unnamed x2, waiting for transfers between devices: 21.2 us -> 2.03 us
    all_gather x1 -> x0, blocking collectives: 13.4 us -> none  [per_device(): lax.all_gather(n_bwd, 'mp', axis=0, tiled=True)]
    ppermute x0 -> x3, waiting for transfers between devices: none -> 8.77 us  [gather_around(): x = lax.ppermute(x, axis, [(d, (d + 1) % ways) for d in range(ways)])]
    ppermute x0 -> x3, starting transfers between devices: none -> 1.97 us  [gather_around(): x = lax.ppermute(x, axis, [(d, (d + 1) % ways) for d in range(ways)])]
  transfers between devices with their start and end apart: 3 -> 6, of which waited for: 1 -> 3; matrix products, arithmetic and copies ran while one was open for 12% -> 36% of each run, Pallas kernels for 0% -> 0%
where the time goes in v1:
time: 161 us; the launch traced here: 160 us
  matrix products  83.9 us (52%)
  blocking collectives  34.1 us (21%)
  between operations  14.8 us (9%)
  waiting for transfers between devices  10.8 us (7%)
  starting transfers between devices  8.17 us (5%)
  other arithmetic  7.29 us (5%)
    dot_general x4, matrix products, contract_rows(): lax.dot_general(left, right, (((0,), (0,)), ((), ())), preferred_element_...  32 us
    dot_general x1, matrix products, per_device(): lax.dot_general(g_fwd, weight_out, (((1,), (1,)), ((), ())), preferred_el...  19.8 us
    all_gather x1, blocking collectives, per_device(): lax.all_gather(n_fwd, 'mp', axis=0, tiled=True)  13.3 us
    all_gather x1, blocking collectives, per_device(): lax.all_gather(upstream, 'mp', axis=0, tiled=True)  13.1 us
    dot_general x1, matrix products, per_device(): lax.dot_general(grad_hidden, weight_in, (((1,), (1,)), ((), ())), preferr...  12.2 us
    dot_general x1, matrix products, per_device(): grad_act = jnp.dot(rows_up, weight_out, preferred_element_type=jnp.float32)  10 us
    dot_general x1, matrix products, per_device(): h_bwd = jnp.dot(rows_bwd, weight_in, preferred_element_type=jnp.float32)  9.92 us
    ppermute x3, waiting for transfers between devices, gather_around(): x = lax.ppermute(x, axis, [(d, (d + 1) % ways) for d in range(ways)])  8.77 us
  transfers between devices with their start and end apart: 6, of which 3 were waited for; matrix products, arithmetic and copies ran while one was open for 36% of the time, Pallas kernels for 0%

profile of v1, /device:TPU:0, one launch (start us, length us, event | category | flops | bytes accessed | tf_op | source)
XLA Modules:
  0.0 160.4 jit_solution(3223563384224370090)
XLA Ops:
  7.2 0.0 all-reduce.5.cloned.1.call-start
  7.2 4.9 %collective-permute-start = (bf16[1,2,3072]{2,1,0:T(2,128)(2,1)}, bf16[1,2,3072]{2,1,0:T(2,128)(2,1)S(1)}, u32[]{:S(2)}, u32[]{:S(2)}) collective-permute-start(bf16[1,2,3072]{2,1,0:T(2,128)(2,1)} %param.8), channel_id=1, source_target_pairs={{0,8},{8,16},{16,24},{1,9},{9,17},{17,25},{2,10},{10,18},{18,26},{... | collective-permute-start | bytes 36872 | tf_op jit(solution)/shard_map/ppermute | solution.py:22
  12.1 1.3 collective-permute-start.1
  13.4 0.8 convert_reduce_fusion.1
  14.2 0.9 fusion.48
  15.2 0.8 constant_dynamic-update-slice_fusion.3
  16.0 1.6 %collective-permute-start.2 = (bf16[2,3072]{1,0:T(2,128)(2,1)S(1)}, bf16[2,3072]{1,0:T(2,128)(2,1)S(1)}, u32[]{:S(2)}, u32[]{:S(2)}) collective-permute-start(bf16[2,3072]{1,0:T(2,128)(2,1)S(1)} %get-tuple-element.9), channel_id=1, source_target_pairs={{0,1},{1,2},{2,3},{3,0},{4,5},{5,6},{6,7},{7,4},{8,9},{9,10},{10,1... | collective-permute-start | bytes 36872 | tf_op jit(solution)/shard_map/ppermute | solution.py:14
  17.6 1.2 dynamic-slice
  19.5 0.0 collective-permute-done
  19.5 0.9 convert_reduce_fusion
  20.4 0.2 fusion.42
  20.6 0.8 fusion.55
  21.4 13.3 %all-gather = bf16[4,2,3072]{2,1,0:T(2,128)(2,1)S(1)} all-gather(bf16[1,2,3072]{2,1,0:T(2,128)(2,1)S(1)} %fusion.55), channel_id=1, replica_groups=mesh['section'=4,'dp'=2,'mp'=4] {'mp'}, dimensions={0}, use_global_device_ids=true | all-gather | bytes 61440 | tf_op jit(solution)/shard_map/all_gather | solution.py:61
  34.7 0.0 copy-start.2
  34.8 19.8 %fusion.2 = f32[8,3072]{1,0:T(8,128)} fusion(bf16[1,3072,4096]{2,1,0:T(8,128)(2,1)} %param.15, bf16[8,3072]{1,0:T(8,128)(2,1)S(1)} %reshape.42, bf16[1,3072,4096]{2,1,0:T(8,128)(2,1)} %param.14), kind=kOutput, calls=%fused_computation.2 | convolution fusion | flops 402948096 | bytes 50479104 | tf_op jit(solution)/shard_map/dot_general | solution.py:69
  54.5 0.0 collective-permute-done.1
  54.5 0.0 copy-done.2
  54.5 13.1 %all-gather.1 = bf16[4,2,3072]{2,1,0:T(2,128)(2,1)S(1)} all-gather(bf16[1,2,3072]{2,1,0:T(2,128)(2,1)S(1)} %fusion.59), channel_id=1, replica_groups=mesh['section'=4,'dp'=2,'mp'=4] {'mp'}, dimensions={0}, use_global_device_ids=true | all-gather | bytes 61440 | tf_op jit(solution)/shard_map/all_gather | solution.py:63
  67.6 0.0 collective-permute-done.2
  67.7 0.3 collective-permute-start.3
  68.0 1.9 %all_gather.22 = bf16[16,3072]{1,0:T(8,128)(2,1)S(1)} all-gather(bf16[8,3072]{1,0:T(8,128)(2,1)S(1)} %reshape.44), channel_id=1, replica_groups=mesh['section'=4,'dp'=2,'mp'=4] {'dp'}, dimensions={0}, use_global_device_ids=true | all-gather | bytes 147456 | tf_op jit(solution)/shard_map/all_gather | solution.py:93
  69.9 3.3 %collective-permute-done.3 = bf16[2,3072]{1,0:T(2,128)(2,1)S(1)} collective-permute-done((bf16[2,3072]{1,0:T(2,128)(2,1)S(1)}, bf16[2,3072]{1,0:T(2,128)(2,1)S(1)}, u32[]{:S(2)}, u32[]{:S(2)}) %collective-permute-start.3) | collective-permute-done | bytes 12320 | tf_op jit(solution)/shard_map/ppermute | solution.py:14
  73.2 0.0 collective-permute-start.4
  73.2 5.5 %collective-permute-done.4 = bf16[2,3072]{1,0:T(2,128)(2,1)S(1)} collective-permute-done((bf16[2,3072]{1,0:T(2,128)(2,1)S(1)}, bf16[2,3072]{1,0:T(2,128)(2,1)S(1)}, u32[]{:S(2)}, u32[]{:S(2)}) %collective-permute-start.4) | collective-permute-done | bytes 12320 | tf_op jit(solution)/shard_map/ppermute | solution.py:14
  78.7 1.9 %all_gather.20 = bf16[16,3072]{1,0:T(8,128)(2,1)S(1)} all-gather(bf16[8,3072]{1,0:T(8,128)(2,1)S(1)} %constant_dynamic-update-slice_fusion), channel_id=1, replica_groups=mesh['section'=4,'dp'=2,'mp'=4] {'dp'}, dimensions={0}, use_global_device_ids=true | all-gather | bytes 147456 | tf_op jit(solution)/shard_map/all_gather | solution.py:92
  80.6 9.9 %multiply_convert_fusion = (bf16[8,4096]{1,0:T(8,128)(2,1)S(1)}, f32[8,4096]{1,0:T(8,128)S(1)}) fusion(bf16[8,3072]{1,0:T(8,128)(2,1)S(1)} %constant_dynamic-update-slice_fusion, bf16[1,3072,4096]{2,1,0:T(8,128)(2,1)} %param.14), kind=kOutput, calls=%fused_computation.33 | convolution fusion | flops 201621504 | bytes 25411584 | tf_op jit(solution)/shard_map/dot_general | solution.py:72
  90.5 10.0 %fusion.15 = bf16[8,4096]{1,0:T(8,128)(2,1)S(1)} fusion(bf16[8,3072]{1,0:T(8,128)(2,1)S(1)} %reshape.44, bf16[1,3072,4096]{2,1,0:T(8,128)(2,1)} %param.15, f32[8,4096]{1,0:T(8,128)S(1)} %get-tuple-element.13), kind=kOutput, calls=%fused_computation.19 | convolution fusion | flops 201949184 | bytes 25411584 | tf_op jit(solution)/shard_map/dot_general | solution.py:75
  100.5 12.2 %fusion.4 = f32[8,3072]{1,0:T(8,128)} fusion(bf16[8,4096]{1,0:T(8,128)(2,1)S(1)} %fusion.15, bf16[1,3072,4096]{2,1,0:T(8,128)(2,1)} %param.14), kind=kOutput, calls=%fused_computation.4 | convolution fusion | flops 201326592 | bytes 25329664 | tf_op jit(solution)/shard_map/dot_general | solution.py:77
  112.7 1.9 %all_gather.21 = bf16[16,4096]{1,0:T(8,128)(2,1)S(1)} all-gather(bf16[8,4096]{1,0:T(8,128)(2,1)S(1)} %fusion.15), channel_id=1, replica_groups=mesh['section'=4,'dp'=2,'mp'=4] {'dp'}, dimensions={0}, use_global_device_ids=true | all-gather | bytes 196608 | tf_op jit(solution)/shard_map/all_gather | solution.py:95
  114.6 2.1 %all_gather.23 = bf16[16,4096]{1,0:T(8,128)(2,1)S(1)} all-gather(bf16[8,4096]{1,0:T(8,128)(2,1)S(1)} %get-tuple-element.12), channel_id=1, replica_groups=mesh['section'=4,'dp'=2,'mp'=4] {'dp'}, dimensions={0}, use_global_device_ids=true | all-gather | bytes 196608 | tf_op jit(solution)/shard_map/all_gather | solution.py:94
  116.7 0.0 all-reduce.5.cloned.1.call-update
  116.7 6.6 %convolution_convert_fusion.3 = bf16[1536,4096]{1,0:T(8,128)(2,1)} fusion(bf16[16,4096]{1,0:T(8,128)(2,1)S(1)} %all_gather.21, bf16[16,3072]{1,0:T(8,128)(2,1)S(1)} %all_gather.20, s32[]{:T(128)S(6)} %select_n.56), kind=kOutput, calls=%fused_computation.15 | convolution fusion | flops 106954752 | bytes 12673028 | tf_op jit(solution)/shard_map/dot_general | solution.py:43
  123.3 9.4 %fusion.10 = bf16[1,1536,4096]{2,1,0:T(8,128)(2,1)} fusion(bf16[1536,4096]{1,0:T(8,128)(2,1)} %convolution_convert_fusion.3, bf16[16,4096]{1,0:T(8,128)(2,1)S(1)} %all_gather.21, bf16[16,3072]{1,0:T(8,128)(2,1)S(1)} %all_gather.20, s32[]{:T(128)S(6)} %add.104, s32[]{:T(128)S(6)} %select_n.56), kind=kOutput, calls=%fused_computation.16 | convolution fusion | flops 132120576 | bytes 25255944 | tf_op jit(solution)/shard_map/dot_general | solution.py:43
  132.7 0.0 copy-start
  132.7 0.0 copy-start.1
  132.7 6.6 %convolution_convert_fusion = bf16[1536,4096]{1,0:T(8,128)(2,1)} fusion(bf16[16,4096]{1,0:T(8,128)(2,1)S(1)} %all_gather.23, bf16[16,3072]{1,0:T(8,128)(2,1)S(1)} %all_gather.22, s32[]{:T(128)S(6)} %add.104, s32[]{:T(128)S(6)} %select_n.56), kind=kOutput, calls=%fused_computation.12 | convolution fusion | flops 106954752 | bytes 12673032 | tf_op jit(solution)/shard_map/dot_general | solution.py:43
  139.3 9.4 %fusion.11 = bf16[1,1536,4096]{2,1,0:T(8,128)(2,1)} fusion(bf16[1536,4096]{1,0:T(8,128)(2,1)} %convolution_convert_fusion, bf16[16,4096]{1,0:T(8,128)(2,1)S(1)} %all_gather.23, bf16[16,3072]{1,0:T(8,128)(2,1)S(1)} %all_gather.22, s32[]{:T(128)S(6)} %select_n.56), kind=kOutput, calls=%fused_computation.17 | convolution fusion | flops 132120576 | bytes 25255940 | tf_op jit(solution)/shard_map/dot_general | solution.py:43
  148.7 2.0 %all-reduce.5.cloned.1.call-done = (f32[8,3072]{1,0:T(8,128)}, f32[8,3072]{1,0:T(8,128)}) async-done(((f32[8,3072]{1,0:T(8,128)}, f32[8,3072]{1,0:T(8,128)}), (f32[8,3072]{1,0:T(8,128)}, f32[8,3072]{1,0:T(8,128)})) %all-reduce.5.cloned.1.call-update) | async-done | bytes 196624
  150.7 0.0 copy-done
  150.7 0.0 copy-done.1
  150.7 1.1 fusion.64
  151.9 1.7 %fusion.54 = (bf16[1,2,3072]{2,1,0:T(2,128)(2,1)}, bf16[1,2,3072]{2,1,0:T(2,128)(2,1)}) fusion(f32[8,3072]{1,0:T(8,128)} %get-tuple-element.6, u32[]{:T(128)S(6)} %multiply.37, bf16[2,3072]{1,0:T(2,128)(2,1)S(1)} %get-tuple-element.11, f32[2]{0:T(128)S(1)} %broadcast_multiply_fusion, f32[2]{0:T(128)S(1)} %broadcast_multiply_fusion.2, ...), kind=kLoop, calls=%fused_computation.67 | loop fusion | flops 92160 | bytes 135205 | tf_op jit(solution)/shard_map/broadcast_in_dim | solution.py:112
  (13 shorter events, 0.2 us)
Async XLA Ops:
  7.2 143.6 %all-reduce.5.cloned.1.call-start = ((), (), s32[]{:S(2)}) async-start(), calls=%async_computation | async-start | bytes 393216
  7.2 12.3 %collective-permute-start = (bf16[1,2,3072]{2,1,0:T(2,128)(2,1)}, bf16[1,2,3072]{2,1,0:T(2,128)(2,1)S(1)}, u32[]{:S(2)}, u32[]{:S(2)}) collective-permute-start(bf16[1,2,3072]{2,1,0:T(2,128)(2,1)} %param.8), channel_id=1, source_target_pairs={{0,8},{8,16},{16,24},{1,9},{9,17},{17,25},{2,10},{10,18},{18,26},{... | collective-permute-start | bytes 36872 | tf_op jit(solution)/shard_map/ppermute | solution.py:22
  12.1 42.4 %collective-permute-start.1 = (bf16[1,2,3072]{2,1,0:T(2,128)(2,1)}, bf16[1,2,3072]{2,1,0:T(2,128)(2,1)S(1)}, u32[]{:S(2)}, u32[]{:S(2)}) collective-permute-start(bf16[1,2,3072]{2,1,0:T(2,128)(2,1)} %param.11), channel_id=1, source_target_pairs={{8,0},{16,8},{24,16},{9,1},{17,9},{25,17},{10,2},{18,10},{26,18},{... | collective-permute-start | bytes 36872 | tf_op jit(solution)/shard_map/ppermute | solution.py:22
  16.0 51.6 %collective-permute-start.2 = (bf16[2,3072]{1,0:T(2,128)(2,1)S(1)}, bf16[2,3072]{1,0:T(2,128)(2,1)S(1)}, u32[]{:S(2)}, u32[]{:S(2)}) collective-permute-start(bf16[2,3072]{1,0:T(2,128)(2,1)S(1)} %get-tuple-element.9), channel_id=1, source_target_pairs={{0,1},{1,2},{2,3},{3,0},{4,5},{5,6},{6,7},{7,4},{8,9},{9,10},{10,1... | collective-permute-start | bytes 36872 | tf_op jit(solution)/shard_map/ppermute | solution.py:14
  34.7 19.8 %copy-start.2 = (bf16[2,3072]{1,0:T(2,128)(2,1)S(1)}, bf16[2,3072]{1,0:T(2,128)(2,1)}, u32[]{:S(2)}) copy-start(bf16[2,3072]{1,0:T(2,128)(2,1)} %param.12) | copy-start | bytes 36868
  67.7 5.5 %collective-permute-start.3 = (bf16[2,3072]{1,0:T(2,128)(2,1)S(1)}, bf16[2,3072]{1,0:T(2,128)(2,1)S(1)}, u32[]{:S(2)}, u32[]{:S(2)}) collective-permute-start(bf16[2,3072]{1,0:T(2,128)(2,1)S(1)} %collective-permute-done.2), channel_id=1, source_target_pairs={{0,1},{1,2},{2,3},{3,0},{4,5},{5,6},{6,7},{7,4},{8,9},{9,10},{10,1... | collective-permute-start | bytes 36872 | tf_op jit(solution)/shard_map/ppermute | solution.py:14
  73.2 5.5 %collective-permute-start.4 = (bf16[2,3072]{1,0:T(2,128)(2,1)S(1)}, bf16[2,3072]{1,0:T(2,128)(2,1)S(1)}, u32[]{:S(2)}, u32[]{:S(2)}) collective-permute-start(bf16[2,3072]{1,0:T(2,128)(2,1)S(1)} %collective-permute-done.3), channel_id=1, source_target_pairs={{0,1},{1,2},{2,3},{3,0},{4,5},{5,6},{6,7},{7,4},{8,9},{9,10},{10,1... | collective-permute-start | bytes 36872 | tf_op jit(solution)/shard_map/ppermute | solution.py:14
  132.7 18.0 %copy-start = (bf16[1,2,3072]{2,1,0:T(2,128)(2,1)S(1)}, bf16[1,2,3072]{2,1,0:T(2,128)(2,1)}, u32[]{:S(2)}) copy-start(bf16[1,2,3072]{2,1,0:T(2,128)(2,1)} %param.10) | copy-start | bytes 36868
  132.7 18.0 %copy-start.1 = (f32[1,3072]{1,0:T(1,128)S(1)}, f32[1,3072]{1,0:T(1,128)}, u32[]{:S(2)}) copy-start(f32[1,3072]{1,0:T(1,128)} %param.13) | copy-start | bytes 36868
Sparse Core Ops, SparseCore 0:
  116.8 33.8 all-reduce.4
